TPU v7x, 256 devices: a whole 4x4x8 slice. The times are simulated.
256 devices in a mesh: row: 32 (over y, x, core), col: 8 (over z).
Axes of the slice: x: 4, y: 4, z: 8, core: 2. Of those that a mesh axis runs over, the one named last changes fastest.
Arguments:
- inputs: bfloat16 [4096, 5120], P('row', 'col'), may hold values from -6 to 6
- grad_out: bfloat16 [4096, 5120], P('row', 'col'), may hold values from -6 to 6
- pre_act: bfloat16 [4096, 13824], P('col', 'row'), may hold values from -6 to 6
- w_in: bfloat16 [13824, 5120], P('row', 'col'), may hold values from -0.078125 to 0.078125
- w_out: bfloat16 [13824, 5120], P('row', 'col'), may hold values from -0.0546875 to 0.0546875
- row_in_prev: float32 [13824], P('row'), may hold values from 204.8 to 24576, as said below
- col_in_prev: float32 [5120], P('col'), may hold values from 204.8 to 24576, as said below
- row_out_prev: float32 [13824], P('row'), may hold values from 204.8 to 24576, as said below
- col_out_prev: float32 [5120], P('col'), may hold values from 204.8 to 24576, as said below
Outputs:
- input_grad: bfloat16 [4096, 5120], P('row', 'col')
- update_in: float32 [13824, 5120], P('row', 'col')
- row_in: float32 [13824], P('row')
- col_in: float32 [5120], P('col')
- update_out: float32 [13824, 5120], P('row', 'col')
- row_out: float32 [13824], P('row')
- col_out: float32 [5120], P('col')
Inputs may be any that keep to these rules, and one draw needn't show every extreme that they name: `row_in_prev`: positive. `col_in_prev`: positive. `row_out_prev`: positive. `col_out_prev`: positive.
All inputs are finite; a program needn't handle non-finite values.
Results may differ from a plain program's by a relative error of at most 0.023.
Values may be sent and summed in bfloat16 or wider, within the bound.
A program may use at most 128 MiB of HBM per device.

v0:
```python
import math
import jax
import jax.numpy as jnp
from jax import lax
from jax.sharding import PartitionSpec as P

D = 5120
FF = 13824
decay_rate = 0.8
epsilon_sq = 1e-30
clip_limit = 0.25
gelu_coef = 0.044715
root_coef = math.sqrt(2.0 / math.pi)


def gelu_parts(pre_float):
    tanh_value = jnp.tanh(root_coef * (pre_float + gelu_coef * pre_float * pre_float * pre_float))
    value = 0.5 * pre_float * (1.0 + tanh_value)
    slope = 0.5 * (1.0 + tanh_value) + 0.5 * pre_float * (
        1.0 - tanh_value * tanh_value
    ) * root_coef * (1.0 + 3.0 * gelu_coef * pre_float * pre_float)
    return (value, slope)


def contract_last(left, right):
    return lax.dot_general(
        left, right, (((1,), (1,)), ((), ())), preferred_element_type=jnp.float32
    )


def contract_first(left, right):
    return lax.dot_general(
        left, right, (((0,), (0,)), ((), ())), preferred_element_type=jnp.float32
    )


def row_moment(row_sum, row_prev):
    return decay_rate * row_prev + (1.0 - decay_rate) * (row_sum / D + epsilon_sq)


def col_moment(col_sum, col_prev):
    return decay_rate * col_prev + (1.0 - decay_rate) * (col_sum / FF + epsilon_sq)


def per_device(
    inputs, grad_out, pre_act, w_in, w_out, row_in_prev, col_in_prev, row_out_prev, col_out_prev
):
    grad_all, input_all = (
        lax.all_gather(grad_out, "row", axis=0, tiled=True),
        lax.all_gather(inputs, "row", axis=0, tiled=True),
    )
    token_count = float(inputs.shape[0] * lax.axis_size("row"))
    rows_here = grad_all
    hidden_grad = lax.psum_scatter(
        contract_last(rows_here, w_out).astype(jnp.bfloat16), "col", scatter_dimension=0, tiled=True
    ).astype(jnp.float32)
    value, slope = gelu_parts(pre_act.astype(jnp.float32))
    act = value.astype(jnp.bfloat16)
    pre_grad = (hidden_grad * slope).astype(jnp.bfloat16)
    act_all, pre_grad_all = (
        lax.all_gather(act, "col", axis=0, tiled=True),
        lax.all_gather(pre_grad, "col", axis=0, tiled=True),
    )
    grad_w_out = contract_first(act_all, grad_all)
    grad_w_in = contract_first(pre_grad_all, input_all)
    rows_here = pre_grad_all
    input_sum = lax.psum_scatter(
        jnp.dot(rows_here, w_in, preferred_element_type=jnp.float32).astype(jnp.bfloat16),
        "row",
        scatter_dimension=0,
        tiled=True,
    )
    square_in = grad_w_in * grad_w_in
    square_out = grad_w_out * grad_w_out
    row_sums = lax.psum((jnp.sum(square_in, axis=1), jnp.sum(square_out, axis=1)), "col")
    row_in = row_moment(row_sums[0], row_in_prev)
    row_out = row_moment(row_sums[1], row_out_prev)
    col_sums = lax.psum((jnp.sum(square_in, axis=0), jnp.sum(square_out, axis=0)), "row")
    col_in = col_moment(col_sums[0], col_in_prev)
    col_out = col_moment(col_sums[1], col_out_prev)
    raw_in = grad_w_in / jnp.sqrt(row_in[:, None] * col_in[None, :] / token_count)
    raw_out = grad_w_out / jnp.sqrt(row_out[:, None] * col_out[None, :] / token_count)
    norms = lax.psum((jnp.sum(raw_in * raw_in), jnp.sum(raw_out * raw_out)), ("row", "col"))
    total_in = norms[0]
    total_out = norms[1]
    rms_in = jnp.sqrt(total_in / (FF * D))
    rms_out = jnp.sqrt(total_out / (FF * D))
    update_in = raw_in / jnp.maximum(1.0, rms_in / clip_limit)
    update_out = raw_out / jnp.maximum(1.0, rms_out / clip_limit)
    return (input_sum, update_in, row_in, col_in, update_out, row_out, col_out)


def solution(mesh):
    return jax.shard_map(
        per_device,
        mesh=mesh,
        in_specs=(
            P("row", "col"),
            P("row", "col"),
            P("col", "row"),
            P("row", "col"),
            P("row", "col"),
            P("row"),
            P("col"),
            P("row"),
            P("col"),
        ),
        out_specs=(
            P("row", "col"),
            P("row", "col"),
            P("row"),
            P("col"),
            P("row", "col"),
            P("row"),
            P("col"),
        ),
        check_vma=False,
    )
```

profile of v0, /device:TPU:1, one launch (start us, length us, event | category | flops | bytes accessed | tf_op | source)
XLA Modules:
  0.0 452.0 jit_solution(9500882296809639069)
XLA Ops:
  7.2 0.0 copy-start
  7.2 0.0 all-gather.5.cloned.1.call-start
  7.2 0.7 all-gather.5.cloned.1.call-update
  7.9 0.0 reduce-scatter.3.cloned.1.call-start
  8.0 59.3 %all-gather.5.cloned.1.call-done = bf16[4096,640]{1,0:T(8,128)(2,1)} async-done(((bf16[128,640]{1,0:T(8,128)(2,1)}), bf16[4096,640]{1,0:T(8,128)(2,1)}) %all-gather.5.cloned.1.call-update) | async-done | bytes 5242896 | tf_op jit(solution)/shard_map/all_gather | solution.py:49
  67.3 7.4 %convolution_convert_fusion.1 = bf16[4096,432]{0,1:T(8,128)(2,1)} fusion(bf16[4096,640]{1,0:T(8,128)(2,1)} %all-gather.5.cloned.1.call-done, bf16[432,640]{1,0:T(8,128)(2,1)} %param.13), kind=kOutput, calls=%fused_computation.1 | convolution fusion | flops 2266693632 | bytes 9334784 | tf_op jit(solution)/shard_map/dot_general | solution.py:26
  74.7 0.0 copy-start.1
  74.7 0.0 reduce-scatter.3.cloned.1.call-update
  74.7 0.0 all-gather.7.cloned.1.call-start
  74.7 48.2 %reduce-scatter.3.cloned.1.call-done = bf16[512,432]{0,1:T(8,128)(2,1)} async-done(((bf16[4096,432]{0,1:T(8,128)(2,1)}), bf16[512,432]{0,1:T(8,128)(2,1)}) %reduce-scatter.3.cloned.1.call-update) | async-done | bytes 442384 | tf_op jit(solution)/shard_map/reduce_scatter | solution.py:54
  123.0 0.0 copy-done.1
  123.0 2.6 fusion.7
  125.6 0.0 all-gather.7.cloned.1.call-update
  125.6 0.0 all-gather.11.cloned.1.call-start
  125.6 0.5 all-gather.11.cloned.1.call-update
  126.2 0.0 all-gather.9.cloned.1.call-start
  126.2 0.5 all-gather.9.cloned.1.call-update
  126.8 0.0 reduce-scatter.5.cloned.1.call-start
  126.8 46.8 %all-gather.7.cloned.1.call-done = bf16[4096,432]{0,1:T(8,128)(2,1)} async-done(((bf16[512,432]{0,1:T(8,128)(2,1)}), bf16[4096,432]{0,1:T(8,128)(2,1)}) %all-gather.7.cloned.1.call-update) | async-done | bytes 3538960 | tf_op jit(solution)/shard_map/all_gather | solution.py:62
  173.6 0.0 copy-done
  173.6 7.9 %convolution_convert_fusion = bf16[4096,640]{1,0:T(8,128)(2,1)} fusion(bf16[4096,432]{0,1:T(8,128)(2,1)} %all-gather.7.cloned.1.call-done, bf16[432,640]{1,0:T(8,128)(2,1)S(1)} %copy-done), kind=kOutput, calls=%fused_computation | convolution fusion | flops 2267545600 | bytes 9334784 | tf_op jit(solution)/shard_map/dot_general | solution.py:68
  181.5 0.0 reduce-scatter.5.cloned.1.call-update
  181.5 41.8 %all-gather.11.cloned.1.call-done = bf16[4096,432]{0,1:T(8,128)(2,1)} async-done(((bf16[512,432]{0,1:T(8,128)(2,1)}), bf16[4096,432]{0,1:T(8,128)(2,1)}) %all-gather.11.cloned.1.call-update) | async-done | bytes 3538960 | tf_op jit(solution)/shard_map/all_gather | solution.py:61
  223.3 6.6 %multiply_reduce_fusion.3 = (f32[432]{0:T(512)S(1)}, f32[640]{0:T(1024)S(1)}, f32[432,640]{1,0:T(8,128)S(1)}) fusion(bf16[4096,432]{0,1:T(8,128)(2,1)} %all-gather.11.cloned.1.call-done, bf16[4096,640]{1,0:T(8,128)(2,1)} %all-gather.5.cloned.1.call-done), kind=kOutput, calls=%fused_computation.16 | convolution fusion | flops 2265752576 | bytes 9892032 | tf_op jit(solution)/shard_map/dot_general | solution.py:32
  229.9 0.0 copy-start.9
  229.9 0.0 copy-start.6
  229.9 0.0 copy-start.7
  229.9 47.6 %all-gather.9.cloned.1.call-done = bf16[4096,640]{1,0:T(8,128)(2,1)} async-done(((bf16[128,640]{1,0:T(8,128)(2,1)}), bf16[4096,640]{1,0:T(8,128)(2,1)}) %all-gather.9.cloned.1.call-update) | async-done | bytes 5242896 | tf_op jit(solution)/shard_map/all_gather | solution.py:50
  277.6 6.6 %multiply_reduce_fusion.5 = (f32[432]{0:T(512)S(1)}, f32[640]{0:T(1024)S(1)}, f32[432,640]{1,0:T(8,128)S(1)}) fusion(bf16[4096,432]{0,1:T(8,128)(2,1)} %all-gather.7.cloned.1.call-done, bf16[4096,640]{1,0:T(8,128)(2,1)} %all-gather.9.cloned.1.call-done), kind=kOutput, calls=%fused_computation.18 | convolution fusion | flops 2265752576 | bytes 9892032 | tf_op jit(solution)/shard_map/dot_general | solution.py:32
  284.1 63.8 %all-reduce.1 = (f32[640]{0:T(1024)S(1)}, f32[640]{0:T(1024)S(1)}) all-reduce(f32[640]{0:T(1024)S(1)} %get-tuple-element.10, f32[640]{0:T(1024)S(1)} %get-tuple-element.8), channel_id=1, replica_groups=mesh['row'=32,'col'=8] {'row'}, use_global_device_ids=true, to_apply=%region_5.0 | all-reduce | flops 1280 | bytes 10240 | tf_op jit(solution)/shard_map/psum | solution.py:78
  347.9 13.8 %all-reduce.2 = (f32[432]{0:T(512)S(1)}, f32[432]{0:T(512)S(1)}) all-reduce(f32[432]{0:T(512)S(1)} %get-tuple-element.9, f32[432]{0:T(512)S(1)} %get-tuple-element.7), channel_id=1, replica_groups=mesh['row'=32,'col'=8] {'col'}, use_global_device_ids=true, to_apply=%region_3.0 | all-reduce | flops 864 | bytes 6912 | tf_op jit(solution)/shard_map/psum | solution.py:75
  361.7 0.0 copy-done.8
  361.7 0.0 copy-done.9
  361.8 0.0 copy-start.4
  361.8 0.0 copy-start.5
  361.8 0.0 copy-done.6
  361.8 0.0 copy-done.7
  361.8 0.0 copy-start.2
  361.8 0.0 copy-start.3
  361.8 1.1 multiply_reduce_fusion
  362.9 1.1 multiply_reduce_fusion.1
  364.0 77.3 %all-reduce = (f32[]{:T(128)}, f32[]{:T(128)}) all-reduce(f32[]{:T(128)} %multiply_reduce_fusion.1, f32[]{:T(128)} %multiply_reduce_fusion), channel_id=1, replica_groups=mesh['row'=32,'col'=8] {'row','col'}, use_global_device_ids=true, to_apply=%region_7.0 | all-reduce | flops 2 | bytes 16 | tf_op jit(solution)/shard_map/psum | solution.py:83
  442.7 0.0 copy-done.4
  442.7 0.0 copy-done.2
  442.7 1.2 fusion.12
  444.0 0.0 copy-done.5
  444.0 0.0 copy-done.3
  444.0 1.2 fusion.11
  (4 shorter events, 0.0 us)
Async XLA Ops:
  7.2 166.5 %copy-start = (bf16[432,640]{1,0:T(8,128)(2,1)S(1)}, bf16[432,640]{1,0:T(8,128)(2,1)}, u32[]{:S(2)}) copy-start(bf16[432,640]{1,0:T(8,128)(2,1)} %param.12) | copy-start | bytes 1658884
  7.2 60.1 %all-gather.5.cloned.1.call-start = ((), (), s32[]{:S(2)}) async-start(), calls=%async_computation.2 | async-start | bytes 5406720 | tf_op jit(solution)/shard_map/all_gather | solution.py:49
  7.9 115.1 %reduce-scatter.3.cloned.1.call-start = ((), (), s32[]{:S(2)}) async-start(), calls=%async_computation.3 | async-start | bytes 3981312 | tf_op jit(solution)/shard_map/reduce_scatter | solution.py:54
  74.7 48.3 %copy-start.1 = (bf16[512,432]{0,1:T(8,128)(2,1)S(1)}, bf16[512,432]{0,1:T(8,128)(2,1)}, u32[]{:S(2)}) copy-start(bf16[512,432]{0,1:T(8,128)(2,1)} %param.11) | copy-start | bytes 1327108
  74.7 98.9 %all-gather.7.cloned.1.call-start = ((), (), s32[]{:S(2)}) async-start(), calls=%async_computation.4 | async-start | bytes 3981312 | tf_op jit(solution)/shard_map/all_gather | solution.py:62
  125.6 97.7 %all-gather.11.cloned.1.call-start = ((), (), s32[]{:S(2)}) async-start(), calls=%async_computation.7 | async-start | bytes 3981312 | tf_op jit(solution)/shard_map/all_gather | solution.py:61
  126.2 151.4 %all-gather.9.cloned.1.call-start = ((), (), s32[]{:S(2)}) async-start(), calls=%async_computation.6 | async-start | bytes 5406720 | tf_op jit(solution)/shard_map/all_gather | solution.py:50
  126.8 318.4 %reduce-scatter.5.cloned.1.call-start = ((), (), s32[]{:S(2)}) async-start(), calls=%async_computation.5 | async-start | bytes 5406720 | tf_op jit(solution)/shard_map/reduce_scatter | solution.py:67
  229.9 131.9 %copy-start.8 = (f32[432]{0:T(512)S(1)}, f32[432]{0:T(512)}, u32[]{:S(2)}) copy-start(f32[432]{0:T(512)} %param.16) | copy-start | bytes 5188
  229.9 131.9 %copy-start.9 = (f32[432]{0:T(512)S(1)}, f32[432]{0:T(512)}, u32[]{:S(2)}) copy-start(f32[432]{0:T(512)} %param.14) | copy-start | bytes 5188
  229.9 131.9 %copy-start.6 = (f32[640]{0:T(1024)S(1)}, f32[640]{0:T(1024)}, u32[]{:S(2)}) copy-start(f32[640]{0:T(1024)} %param.17) | copy-start | bytes 7684
  229.9 131.9 %copy-start.7 = (f32[640]{0:T(1024)S(1)}, f32[640]{0:T(1024)}, u32[]{:S(2)}) copy-start(f32[640]{0:T(1024)} %param.15) | copy-start | bytes 7684
  361.8 80.9 %copy-start.4 = (f32[432]{0:T(512)}, f32[432]{0:T(512)S(1)}, u32[]{:S(2)}) copy-start(f32[432]{0:T(512)S(1)} %get-tuple-element.23) | copy-start | bytes 5188
  361.8 82.2 %copy-start.5 = (f32[432]{0:T(512)}, f32[432]{0:T(512)S(1)}, u32[]{:S(2)}) copy-start(f32[432]{0:T(512)S(1)} %get-tuple-element.24) | copy-start | bytes 5188
  361.8 80.9 %copy-start.2 = (f32[640]{0:T(1024)}, f32[640]{0:T(1024)S(1)}, u32[]{:S(2)}) copy-start(f32[640]{0:T(1024)S(1)} %get-tuple-element.21) | copy-start | bytes 7684
  361.8 82.1 %copy-start.3 = (f32[640]{0:T(1024)}, f32[640]{0:T(1024)S(1)}, u32[]{:S(2)}) copy-start(f32[640]{0:T(1024)S(1)} %get-tuple-element.22) | copy-start | bytes 7684
Sparse Core Ops, SparseCore 0:
  10.6 56.6 all-gather.4
  74.8 48.1 reduce-scatter.2
  125.7 47.8 all-gather.6
  176.0 47.2 all-gather.10
  226.0 51.4 all-gather.8
  282.5 89.6 reduce-scatter.4
where the time goes:
time: 452 us
  waiting for transfers between devices  246 us (54%)
  blocking collectives  155 us (34%)
  matrix products  28.4 us (6%)
  between operations  15.6 us (3%)
  other arithmetic  7.26 us (2%)
    psum x1, blocking collectives, per_device(): lax.psum((jnp.sum(raw_in * raw_in), jnp.sum(raw_out * raw_out)), ('row',...  77.3 us
    psum x1, blocking collectives, per_device(): lax.psum((jnp.sum(square_in, axis=0), jnp.sum(square_out, axis=0)), 'row')  63.8 us
    all_gather x1, waiting for transfers between devices, per_device(): lax.all_gather(grad_out, 'row', axis=0, tiled=True)  59.3 us
    reduce_scatter x1, waiting for transfers between devices, per_device(): lax.psum_scatter(contract_last(rows_here, w_out).astype(jnp.bfloat16), 'c...  48.2 us
    all_gather x1, waiting for transfers between devices, per_device(): lax.all_gather(inputs, 'row', axis=0, tiled=True)  47.6 us
    all_gather x1, waiting for transfers between devices, per_device(): lax.all_gather(pre_grad, 'col', axis=0, tiled=True)  46.8 us
    all_gather x1, waiting for transfers between devices, per_device(): lax.all_gather(act, 'col', axis=0, tiled=True)  41.8 us
    psum x1, blocking collectives, per_device(): lax.psum((jnp.sum(square_in, axis=1), jnp.sum(square_out, axis=1)), 'col')  13.8 us
  transfers between devices with their start and end apart: 6, of which 5 were waited for; matrix products, arithmetic and copies ran while one was open for 6% of the time, Pallas kernels for 0%

commit v1 on v0

--- a/solution.py
+++ b/solution.py
@@ -11,6 +11,19 @@
 clip_limit = 0.25
 gelu_coef = 0.044715
 root_coef = math.sqrt(2.0 / math.pi)
+
+
+def gather_around(array, axis, dim):
+    ways = lax.axis_size(axis)
+    up = [(d, (d + 1) % ways) for d in range(ways)]
+    down = [(d, (d - 1) % ways) for d in range(ways)]
+    earlier, later = ([array], [array])
+    for _ in range(ways // 2):
+        earlier.append(lax.ppermute(earlier[-1], axis, up))
+    for _ in range((ways - 1) // 2):
+        later.append(lax.ppermute(later[-1], axis, down))
+    line = jnp.concatenate([*earlier[::-1], *later[1:]], axis=dim)
+    return jnp.roll(line, (lax.axis_index(axis) - ways // 2) * array.shape[dim], axis=dim)
 
 
 def gelu_parts(pre_float):
@@ -59,7 +72,7 @@
     pre_grad = (hidden_grad * slope).astype(jnp.bfloat16)
     act_all, pre_grad_all = (
         lax.all_gather(act, "col", axis=0, tiled=True),
-        lax.all_gather(pre_grad, "col", axis=0, tiled=True),
+        gather_around(pre_grad, "col", 0),
     )
     grad_w_out = contract_first(act_all, grad_all)
     grad_w_in = contract_first(pre_grad_all, input_all)

time: 452 us -> 403 us (0.89)
  waiting for transfers between devices: 246 us -> 185 us
  starting transfers between devices: 0.24 us -> 8.31 us
  local copies, waits for them, and re-layouts: 0.06 us -> 5.98 us
    all_gather x1, waiting for transfers between devices: 47.6 us -> 0.02 us  [per_device(): lax.all_gather(inputs, 'row', axis=0, tiled=True)]
    all_gather x1 -> x0, waiting for transfers between devices: 46.8 us -> none  [per_device(): lax.all_gather(pre_grad, 'col', axis=0, tiled=True)]
    ppermute x0 -> x7, waiting for transfers between devices: none -> 35.7 us  [the longest x4 35.7 us: gather_around(): earlier.append(lax.ppermute(earlier[-1], axis, up))]
    ppermute x0 -> x7, starting transfers between devices: none -> 8.11 us  [the longest x3 8.02 us: gather_around(): later.append(lax.ppermute(later[-1], axis, down))]
    unnamed x20 -> x37, local copies, waits for them, and re-layouts: 0.06 us -> 5.93 us
  transfers between devices with their start and end apart: 6 -> 12, of which waited for: 5 -> 7; matrix products, arithmetic and copies ran while one was open for 6% -> 7% of each run, Pallas kernels for 0% -> 0%
where the time goes in v1:
time: 403 us; the launch traced here: 402 us
  waiting for transfers between devices  185 us (46%)
  blocking collectives  155 us (38%)
  matrix products  25.7 us (6%)
  between operations  15.5 us (4%)
  starting transfers between devices  8.31 us (2%)
  other arithmetic  7.12 us (2%)
  local copies, waits for them, and re-layouts  5.98 us (1%)
    psum x1, blocking collectives, per_device(): lax.psum((jnp.sum(raw_in * raw_in), jnp.sum(raw_out * raw_out)), ('row',...  79.4 us
    psum x1, blocking collectives, per_device(): lax.psum((jnp.sum(square_in, axis=0), jnp.sum(square_out, axis=0)), 'row')  64 us
    all_gather x1, waiting for transfers between devices, per_device(): lax.all_gather(grad_out, 'row', axis=0, tiled=True)  59.3 us
    reduce_scatter x1, waiting for transfers between devices, per_device(): lax.psum_scatter(contract_last(rows_here, w_out).astype(jnp.bfloat16), 'c...  47.5 us
    all_gather x1, waiting for transfers between devices, per_device(): lax.all_gather(act, 'col', axis=0, tiled=True)  40.7 us
    ppermute x4, waiting for transfers between devices, gather_around(): earlier.append(lax.ppermute(earlier[-1], axis, up))  35.7 us
    dot_general x2, matrix products, contract_first(): lax.dot_general(left, right, (((0,), (0,)), ((), ())), preferred_element_...  13.1 us
    psum x1, blocking collectives, per_device(): lax.psum((jnp.sum(square_in, axis=1), jnp.sum(square_out, axis=1)), 'col')  11.6 us
  transfers between devices with their start and end apart: 12, of which 7 were waited for; matrix products, arithmetic and copies ran while one was open for 7% of the time, Pallas kernels for 0%

profile of v1, /device:TPU:1, one launch (start us, length us, event | category | flops | bytes accessed | tf_op | source)
XLA Modules:
  0.0 402.3 jit_solution(14158970346454375787)
XLA Ops:
  7.2 0.0 all-gather.4.cloned.1.call-start
  7.2 0.7 all-gather.4.cloned.1.call-update
  7.9 0.0 reduce-scatter.3.cloned.1.call-start
  8.0 59.3 %all-gather.4.cloned.1.call-done = bf16[4096,640]{1,0:T(8,128)(2,1)} async-done(((bf16[128,640]{1,0:T(8,128)(2,1)}), bf16[4096,640]{1,0:T(8,128)(2,1)}) %all-gather.4.cloned.1.call-update) | async-done | bytes 5242896 | tf_op jit(solution)/shard_map/all_gather | solution.py:62
  67.3 7.3 %convolution_convert_fusion.1 = bf16[4096,432]{0,1:T(8,128)(2,1)} fusion(bf16[4096,640]{1,0:T(8,128)(2,1)} %all-gather.4.cloned.1.call-done, bf16[432,640]{1,0:T(8,128)(2,1)} %param.13), kind=kOutput, calls=%fused_computation.1 | convolution fusion | flops 2266693632 | bytes 9334784 | tf_op jit(solution)/shard_map/dot_general | solution.py:39
  74.6 0.0 reduce-scatter.3.cloned.1.call-update
  74.6 0.0 all-gather.6.cloned.1.call-start
  74.7 0.7 all-gather.6.cloned.1.call-update
  75.4 0.0 all-gather.8.cloned.1.call-start
  75.4 47.5 %reduce-scatter.3.cloned.1.call-done = bf16[512,432]{0,1:T(8,128)(2,1)} async-done(((bf16[4096,432]{0,1:T(8,128)(2,1)}), bf16[512,432]{0,1:T(8,128)(2,1)}) %reduce-scatter.3.cloned.1.call-update) | async-done | bytes 442384 | tf_op jit(solution)/shard_map/reduce_scatter | solution.py:67
  122.9 2.4 fusion.10
  125.4 0.0 reduce-scatter.5.cloned.1.call-start
  125.4 0.1 collective-permute-start
  125.5 12.3 %collective-permute-done = bf16[512,432]{0,1:T(8,128)(2,1)S(1)} collective-permute-done((bf16[512,432]{0,1:T(8,128)(2,1)S(1)}, bf16[512,432]{0,1:T(8,128)(2,1)S(1)}, u32[]{:S(2)}, u32[]{:S(2)}) %collective-permute-start) | collective-permute-done | bytes 442400 | tf_op jit(solution)/shard_map/ppermute | solution.py:22
  137.8 2.7 collective-permute-start.4
  140.5 8.7 %collective-permute-done.1 = bf16[512,432]{0,1:T(8,128)(2,1)S(1)} collective-permute-done((bf16[512,432]{0,1:T(8,128)(2,1)S(1)}, bf16[512,432]{0,1:T(8,128)(2,1)S(1)}, u32[]{:S(2)}, u32[]{:S(2)}) %collective-permute-start.1) | collective-permute-done | bytes 442400 | tf_op jit(solution)/shard_map/ppermute | solution.py:22
  149.2 2.7 collective-permute-start.5
  151.9 7.8 %collective-permute-done.2 = bf16[512,432]{0,1:T(8,128)(2,1)S(1)} collective-permute-done((bf16[512,432]{0,1:T(8,128)(2,1)S(1)}, bf16[512,432]{0,1:T(8,128)(2,1)S(1)}, u32[]{:S(2)}, u32[]{:S(2)}) %collective-permute-start.2) | collective-permute-done | bytes 442400 | tf_op jit(solution)/shard_map/ppermute | solution.py:22
  159.7 2.7 collective-permute-start.6
  162.3 7.0 %collective-permute-done.3 = bf16[512,432]{0,1:T(8,128)(2,1)} collective-permute-done((bf16[512,432]{0,1:T(8,128)(2,1)S(1)}, bf16[512,432]{0,1:T(8,128)(2,1)}, u32[]{:S(2)}, u32[]{:S(2)}) %collective-permute-start.3) | collective-permute-done | bytes 442400 | tf_op jit(solution)/shard_map/ppermute | solution.py:22
  169.3 1.1 constant_dynamic-update-slice_fusion.15
  170.4 0.1 constant_dynamic-update-slice_fusion.14
  170.5 0.1 constant_dynamic-update-slice_fusion.13
  170.6 0.1 constant_dynamic-update-slice_fusion.12
  170.6 0.1 constant_dynamic-update-slice_fusion.11
  170.7 0.1 constant_dynamic-update-slice_fusion.10
  170.7 0.1 constant_dynamic-update-slice_fusion.9
  170.9 1.1 constant_dynamic-update-slice_fusion.7
  172.0 0.1 constant_dynamic-update-slice_fusion.6
  172.0 0.1 constant_dynamic-update-slice_fusion.5
  172.1 0.1 constant_dynamic-update-slice_fusion.4
  172.2 0.1 constant_dynamic-update-slice_fusion.3
  172.2 0.1 constant_dynamic-update-slice_fusion.2
  172.3 0.1 constant_dynamic-update-slice_fusion.1
  172.4 0.1 constant_dynamic-update-slice_fusion
  172.4 2.9 copy-done.4
  175.4 5.2 %convolution_convert_fusion = bf16[4096,640]{1,0:T(8,128)(2,1)} fusion(bf16[432,640]{1,0:T(8,128)(2,1)S(1)} %copy-done, bf16[8192,432]{0,1:T(8,128)(2,1)S(1)} %constant_dynamic-update-slice_fusion, s32[]{:T(128)S(6)} %select_n.14), kind=kOutput, calls=%fused_computation | convolution fusion | flops 2267545600 | bytes 9334788 | tf_op jit(solution)/shard_map/dot_general | solution.py:81
  180.6 0.0 all-gather.6.cloned.1.call-done
  180.6 6.6 %multiply_reduce_fusion.5 = (f32[432]{0:T(512)S(1)}, f32[640]{0:T(1024)S(1)}, f32[432,640]{1,0:T(8,128)S(1)}) fusion(bf16[4096,640]{1,0:T(8,128)(2,1)} %all-gather.6.cloned.1.call-done, bf16[8192,432]{0,1:T(8,128)(2,1)} %copy-done.4, s32[]{:T(128)S(6)} %select_n.14), kind=kOutput, calls=%fused_computation.21 | convolution fusion | flops 2265752576 | bytes 9892036 | tf_op jit(solution)/shard_map/dot_general | solution.py:45
  187.3 40.7 %all-gather.8.cloned.1.call-done = bf16[4096,432]{0,1:T(8,128)(2,1)} async-done(((bf16[512,432]{0,1:T(8,128)(2,1)}), bf16[4096,432]{0,1:T(8,128)(2,1)}) %all-gather.8.cloned.1.call-update) | async-done | bytes 3538960 | tf_op jit(solution)/shard_map/all_gather | solution.py:74
  228.0 6.6 %multiply_reduce_fusion.3 = (f32[432]{0:T(512)S(1)}, f32[640]{0:T(1024)S(1)}, f32[432,640]{1,0:T(8,128)S(1)}) fusion(bf16[4096,432]{0,1:T(8,128)(2,1)} %all-gather.8.cloned.1.call-done, bf16[4096,640]{1,0:T(8,128)(2,1)} %all-gather.4.cloned.1.call-done), kind=kOutput, calls=%fused_computation.19 | convolution fusion | flops 2265752576 | bytes 9892032 | tf_op jit(solution)/shard_map/dot_general | solution.py:45
  234.5 64.0 %all-reduce.1 = (f32[640]{0:T(1024)S(1)}, f32[640]{0:T(1024)S(1)}) all-reduce(f32[640]{0:T(1024)S(1)} %get-tuple-element.10, f32[640]{0:T(1024)S(1)} %get-tuple-element.8), channel_id=1, replica_groups=mesh['row'=32,'col'=8] {'row'}, use_global_device_ids=true, to_apply=%region_5.6 | all-reduce | flops 1280 | bytes 10240 | tf_op jit(solution)/shard_map/psum | solution.py:91
  298.6 11.6 %all-reduce.2 = (f32[432]{0:T(512)S(1)}, f32[432]{0:T(512)S(1)}) all-reduce(f32[432]{0:T(512)S(1)} %get-tuple-element.9, f32[432]{0:T(512)S(1)} %get-tuple-element.7), channel_id=1, replica_groups=mesh['row'=32,'col'=8] {'col'}, use_global_device_ids=true, to_apply=%region_3.4 | all-reduce | flops 864 | bytes 6912 | tf_op jit(solution)/shard_map/psum | solution.py:88
  310.3 1.1 multiply_reduce_fusion
  311.4 1.1 multiply_reduce_fusion.1
  312.5 79.4 %all-reduce = (f32[]{:T(128)}, f32[]{:T(128)}) all-reduce(f32[]{:T(128)} %multiply_reduce_fusion.1, f32[]{:T(128)} %multiply_reduce_fusion), channel_id=1, replica_groups=mesh['row'=32,'col'=8] {'row','col'}, use_global_device_ids=true, to_apply=%region_7.8 | all-reduce | flops 2 | bytes 16 | tf_op jit(solution)/shard_map/psum | solution.py:96
  393.3 1.2 fusion.15
  394.5 1.2 fusion.14
  (33 shorter events, 0.2 us)
Async XLA Ops:
  7.2 168.2 %copy-start = (bf16[432,640]{1,0:T(8,128)(2,1)S(1)}, bf16[432,640]{1,0:T(8,128)(2,1)}, u32[]{:S(2)}) copy-start(bf16[432,640]{1,0:T(8,128)(2,1)} %param.12) | copy-start | bytes 1658884
  7.2 60.1 %all-gather.4.cloned.1.call-start = ((), (), s32[]{:S(2)}) async-start(), calls=%async_computation.2 | async-start | bytes 5406720 | tf_op jit(solution)/shard_map/all_gather | solution.py:62
  7.9 115.0 %copy-start.1 = (bf16[512,432]{0,1:T(8,128)(2,1)S(1)}, bf16[512,432]{0,1:T(8,128)(2,1)}, u32[]{:S(2)}) copy-start(bf16[512,432]{0,1:T(8,128)(2,1)} %param.11) | copy-start | bytes 1327108
  7.9 115.0 %reduce-scatter.3.cloned.1.call-start = ((), (), s32[]{:S(2)}) async-start(), calls=%async_computation.3 | async-start | bytes 3981312 | tf_op jit(solution)/shard_map/reduce_scatter | solution.py:67
  74.6 106.0 %all-gather.6.cloned.1.call-start = ((), (), s32[]{:S(2)}) async-start(), calls=%async_computation.5 | async-start | bytes 5406720 | tf_op jit(solution)/shard_map/all_gather | solution.py:63
  75.4 152.6 %all-gather.8.cloned.1.call-start = ((), (), s32[]{:S(2)}) async-start(), calls=%async_computation.6 | async-start | bytes 3981312 | tf_op jit(solution)/shard_map/all_gather | solution.py:74
  125.4 270.4 %reduce-scatter.5.cloned.1.call-start = ((), (), s32[]{:S(2)}) async-start(), calls=%async_computation.4 | async-start | bytes 5406720 | tf_op jit(solution)/shard_map/reduce_scatter | solution.py:80
  125.4 12.4 %collective-permute-start = (bf16[512,432]{0,1:T(8,128)(2,1)S(1)}, bf16[512,432]{0,1:T(8,128)(2,1)S(1)}, u32[]{:S(2)}, u32[]{:S(2)}) collective-permute-start(bf16[512,432]{0,1:T(8,128)(2,1)S(1)} %get-tuple-element.18), channel_id=1, source_target_pairs={{0,1},{1,2},{2,3},{3,4},{4,5},{5,6},{6,7},{7,0},{8,9},{9,10},{10,1... | collective-permute-start | bytes 1327112 | tf_op jit(solution)/shard_map/ppermute | solution.py:22
  137.8 11.4 %collective-permute-start.1 = (bf16[512,432]{0,1:T(8,128)(2,1)S(1)}, bf16[512,432]{0,1:T(8,128)(2,1)S(1)}, u32[]{:S(2)}, u32[]{:S(2)}) collective-permute-start(bf16[512,432]{0,1:T(8,128)(2,1)S(1)} %collective-permute-done), channel_id=1, source_target_pairs={{0,1},{1,2},{2,3},{3,4},{4,5},{5,6},{6,7},{7,0},{8,9},{9,10},{10,1... | collective-permute-start | bytes 1327112 | tf_op jit(solution)/shard_map/ppermute | solution.py:22
  137.8 11.4 %collective-permute-start.4 = (bf16[512,432]{0,1:T(8,128)(2,1)S(1)}, bf16[512,432]{0,1:T(8,128)(2,1)S(1)}, u32[]{:S(2)}, u32[]{:S(2)}) collective-permute-start(bf16[512,432]{0,1:T(8,128)(2,1)S(1)} %get-tuple-element.18), channel_id=1, source_target_pairs={{0,7},{1,0},{2,1},{3,2},{4,3},{5,4},{6,5},{7,6},{8,15},{9,8},{10,9... | collective-permute-start | bytes 1327112 | tf_op jit(solution)/shard_map/ppermute | solution.py:24
  149.2 10.5 %collective-permute-start.2 = (bf16[512,432]{0,1:T(8,128)(2,1)S(1)}, bf16[512,432]{0,1:T(8,128)(2,1)S(1)}, u32[]{:S(2)}, u32[]{:S(2)}) collective-permute-start(bf16[512,432]{0,1:T(8,128)(2,1)S(1)} %collective-permute-done.1), channel_id=1, source_target_pairs={{0,1},{1,2},{2,3},{3,4},{4,5},{5,6},{6,7},{7,0},{8,9},{9,10},{10,1... | collective-permute-start | bytes 1327112 | tf_op jit(solution)/shard_map/ppermute | solution.py:22
  149.2 10.5 %collective-permute-start.5 = (bf16[512,432]{0,1:T(8,128)(2,1)S(1)}, bf16[512,432]{0,1:T(8,128)(2,1)S(1)}, u32[]{:S(2)}, u32[]{:S(2)}) collective-permute-start(bf16[512,432]{0,1:T(8,128)(2,1)S(1)} %collective-permute-done.4), channel_id=1, source_target_pairs={{0,7},{1,0},{2,1},{3,2},{4,3},{5,4},{6,5},{7,6},{8,15},{9,8},{10,9... | collective-permute-start | bytes 1327112 | tf_op jit(solution)/shard_map/ppermute | solution.py:24
  159.6 9.6 %collective-permute-start.3 = (bf16[512,432]{0,1:T(8,128)(2,1)S(1)}, bf16[512,432]{0,1:T(8,128)(2,1)}, u32[]{:S(2)}, u32[]{:S(2)}) collective-permute-start(bf16[512,432]{0,1:T(8,128)(2,1)S(1)} %collective-permute-done.2), channel_id=1, source_target_pairs={{0,1},{1,2},{2,3},{3,4},{4,5},{5,6},{6,7},{7,0},{8,9},{9,10},{10,1... | collective-permute-start | bytes 1327112 | tf_op jit(solution)/shard_map/ppermute | solution.py:22
  159.7 11.2 %collective-permute-start.6 = (bf16[512,432]{0,1:T(8,128)(2,1)S(1)}, bf16[512,432]{0,1:T(8,128)(2,1)S(1)}, u32[]{:S(2)}, u32[]{:S(2)}) collective-permute-start(bf16[512,432]{0,1:T(8,128)(2,1)S(1)} %collective-permute-done.5), channel_id=1, source_target_pairs={{0,7},{1,0},{2,1},{3,2},{4,3},{5,4},{6,5},{7,6},{8,15},{9,8},{10,9... | collective-permute-start | bytes 1327112 | tf_op jit(solution)/shard_map/ppermute | solution.py:24
  172.4 2.9 copy-start.4
  187.2 123.0 %copy-start.9 = (f32[432]{0:T(512)S(1)}, f32[432]{0:T(512)}, u32[]{:S(2)}) copy-start(f32[432]{0:T(512)} %param.16) | copy-start | bytes 5188
  187.2 123.0 %copy-start.10 = (f32[432]{0:T(512)S(1)}, f32[432]{0:T(512)}, u32[]{:S(2)}) copy-start(f32[432]{0:T(512)} %param.14) | copy-start | bytes 5188
  187.2 123.0 %copy-start.7 = (f32[640]{0:T(1024)S(1)}, f32[640]{0:T(1024)}, u32[]{:S(2)}) copy-start(f32[640]{0:T(1024)} %param.17) | copy-start | bytes 7684
  187.3 123.0 %copy-start.8 = (f32[640]{0:T(1024)S(1)}, f32[640]{0:T(1024)}, u32[]{:S(2)}) copy-start(f32[640]{0:T(1024)} %param.15) | copy-start | bytes 7684
  310.2 85.5 %copy-start.5 = (f32[432]{0:T(512)}, f32[432]{0:T(512)S(1)}, u32[]{:S(2)}) copy-start(f32[432]{0:T(512)S(1)} %get-tuple-element.23) | copy-start | bytes 5188
  310.2 85.5 %copy-start.6 = (f32[432]{0:T(512)}, f32[432]{0:T(512)S(1)}, u32[]{:S(2)}) copy-start(f32[432]{0:T(512)S(1)} %get-tuple-element.24) | copy-start | bytes 5188
  310.3 85.5 %copy-start.2 = (f32[640]{0:T(1024)}, f32[640]{0:T(1024)S(1)}, u32[]{:S(2)}) copy-start(f32[640]{0:T(1024)S(1)} %get-tuple-element.21) | copy-start | bytes 7684
  310.3 85.5 %copy-start.3 = (f32[640]{0:T(1024)}, f32[640]{0:T(1024)S(1)}, u32[]{:S(2)}) copy-start(f32[640]{0:T(1024)S(1)} %get-tuple-element.22) | copy-start | bytes 7684
Sparse Core Ops, SparseCore 0:
  10.6 56.6 all-gather.3
  74.7 48.1 reduce-scatter.2
  125.8 52.0 all-gather.5
  180.3 47.6 all-gather.7
  232.9 89.1 reduce-scatter.4
